TPU v7x, 256 devices: a whole 4x4x8 slice. The times are simulated.
256 devices in a mesh: seq: 32 (over z, y), head: 8 (over x, core).
Axes of the slice: x: 4, y: 4, z: 8, core: 2. Of those that a mesh axis runs over, the one named last changes fastest.
Arguments:
- query: bfloat16 [16384, 6144], P('seq', 'head'), may hold values from -6 to 6
- key: bfloat16 [16384, 6144], P('seq', 'head'), may hold values from -6 to 6
- value: bfloat16 [16384, 6144], P('seq', 'head'), may hold values from -6 to 6
- init_state: float32 [48, 128, 128], P('head'), may hold values from -768 to 768
- out_weight: bfloat16 [6144, 6144], P(('head', 'seq')), may hold values from -0.078125 to 0.078125
- out_grad: bfloat16 [16384, 6144], P('seq'), may hold values from -24 to 24
Outputs:
- mixed: bfloat16 [16384, 6144], P('seq', 'head')
- grad_query: bfloat16 [16384, 6144], P('seq', 'head')
- grad_key: bfloat16 [16384, 6144], P('seq', 'head')
- grad_value: bfloat16 [16384, 6144], P('seq', 'head')
- init_grad: float32 [48, 128, 128], P('head')
All inputs are finite; a program needn't handle non-finite values.
Results may differ from a plain program's by a relative error of at most 0.017.
Values may be sent and summed in bfloat16 or wider, within the bound.
A program may use at most 128 MiB of HBM per device.

v0:
```python
import jax
import jax.numpy as jnp
from jax import lax
from jax.sharding import PartitionSpec as P

EPS = 1e-06


def prefix(value, axis, join, neutral, backward):
    count = lax.axis_size(axis)
    place = lax.axis_index(axis)
    ahead = count - 1 - place if backward else place
    gathered = lax.all_gather(value.astype(jnp.bfloat16), axis)
    state = jnp.zeros_like(value) + jnp.asarray(neutral, value.dtype)

    def one(turn, state):
        source = count - 1 - turn if backward else turn
        return join(state, lax.dynamic_index_in_dim(gathered, source, 0, False).astype(value.dtype))

    return lax.fori_loop(0, ahead, one, state)


def normalize(attended):
    return attended * lax.rsqrt(jnp.mean(attended * attended, axis=-1, keepdims=True) + EPS)


def add_states(earlier, later):
    return earlier + later


def shards(query, key, value, init_state, out_weight, out_grad):
    tok_rows = query.shape[0]
    width = query.shape[1]
    heads_here = init_state.shape[0]
    head_dim = init_state.shape[2]
    queries = query.reshape(tok_rows, heads_here, head_dim)
    key_rows = key.reshape(tok_rows, heads_here, head_dim)
    val_rows = value.reshape(tok_rows, heads_here, head_dim)
    local_state = jnp.einsum("thi,thj->hij", key_rows, val_rows, preferred_element_type=jnp.float32)
    zero_state = jnp.zeros_like(local_state)
    earlier = prefix(local_state, "seq", add_states, zero_state, False)
    state_half = (init_state + earlier).astype(jnp.bfloat16)
    row_index = lax.broadcasted_iota(jnp.int32, (tok_rows, tok_rows), 0)
    col_index = lax.broadcasted_iota(jnp.int32, (tok_rows, tok_rows), 1)
    causal = col_index <= row_index
    scores = jnp.einsum("thi,shi->hts", queries, key_rows, preferred_element_type=jnp.float32)
    attn_weights = jnp.where(causal, scores, 0.0).astype(jnp.bfloat16)
    attended = jnp.einsum(
        "hts,shj->thj", attn_weights, val_rows, preferred_element_type=jnp.float32
    )
    attended = attended + jnp.einsum(
        "thi,hij->thj", queries, state_half, preferred_element_type=jnp.float32
    )
    normed = normalize(attended).astype(jnp.bfloat16).reshape(tok_rows, width)
    weight_rows = lax.all_gather(out_weight, "seq", axis=0, tiled=True)
    projected = jnp.dot(normed, weight_rows, preferred_element_type=jnp.float32)
    grad_normed = lax.dot_general(
        out_grad, weight_rows, (((1,), (1,)), ((), ())), preferred_element_type=jnp.float32
    )
    mixed = lax.psum_scatter(
        projected.astype(jnp.bfloat16), "head", scatter_dimension=1, tiled=True
    )
    _, norm_back = jax.vjp(normalize, attended)
    grad_att = norm_back(grad_normed.reshape(tok_rows, heads_here, head_dim))[0].astype(
        jnp.bfloat16
    )
    grad_scores = jnp.einsum("thj,shj->hts", grad_att, val_rows, preferred_element_type=jnp.float32)
    grad_scores = jnp.where(causal, grad_scores, 0.0).astype(jnp.bfloat16)
    own_adjoint = jnp.einsum("thi,thj->hij", queries, grad_att, preferred_element_type=jnp.float32)
    later = prefix(own_adjoint, "seq", add_states, zero_state, True)
    later_half = later.astype(jnp.bfloat16)
    grad_query = jnp.einsum(
        "hts,shi->thi", grad_scores, key_rows, preferred_element_type=jnp.float32
    )
    grad_query = grad_query + jnp.einsum(
        "thj,hij->thi", grad_att, state_half, preferred_element_type=jnp.float32
    )
    grad_key = jnp.einsum("hts,thi->shi", grad_scores, queries, preferred_element_type=jnp.float32)
    grad_key = grad_key + jnp.einsum(
        "thj,hij->thi", val_rows, later_half, preferred_element_type=jnp.float32
    )
    grad_value = jnp.einsum(
        "hts,thj->shj", attn_weights, grad_att, preferred_element_type=jnp.float32
    )
    grad_value = grad_value + jnp.einsum(
        "thi,hij->thj", key_rows, later_half, preferred_element_type=jnp.float32
    )
    init_grad = lax.psum(own_adjoint.astype(jnp.bfloat16), "seq").astype(jnp.float32)
    return (
        mixed,
        grad_query.reshape(tok_rows, width).astype(jnp.bfloat16),
        grad_key.reshape(tok_rows, width).astype(jnp.bfloat16),
        grad_value.reshape(tok_rows, width).astype(jnp.bfloat16),
        init_grad,
    )


def solution(mesh):
    return jax.shard_map(
        shards,
        mesh=mesh,
        in_specs=(
            P("seq", "head"),
            P("seq", "head"),
            P("seq", "head"),
            P("head", None, None),
            P(("head", "seq"), None),
            P("seq", None),
        ),
        out_specs=(
            P("seq", "head"),
            P("seq", "head"),
            P("seq", "head"),
            P("seq", "head"),
            P("head", None, None),
        ),
        check_vma=False,
    )
```

profile of v0, /device:TPU:1, one launch (start us, length us, event | category | flops | bytes accessed | tf_op | source)
XLA Modules:
  0.0 504.5 jit_solution(3683059020974468242)
XLA Ops:
  7.2 1.5 copy.55
  8.7 1.4 copy.58
  10.1 1.0 convolution_convert_fusion.2
  12.3 1.1 select_convert_fusion.1
  13.5 1.7 copy-done
  15.1 2.3 fusion.7
  17.4 86.1 %all-gather.8.cloned.1.call-done = bf16[192,128,128]{2,1,0:T(8,128)(2,1)} async-done(((bf16[6,128,128]{2,1,0:T(8,128)(2,1)}), bf16[192,128,128]{2,1,0:T(8,128)(2,1)}) %all-gather.8.cloned.1.call-update) | async-done | bytes 6291472 | tf_op jit(solution)/shard_map/all_gather | solution.py:13
  103.6 102.9 %all-gather.6.cloned.1.call-done = bf16[768,6144]{1,0:T(8,128)(2,1)} async-done(((bf16[24,6144]{1,0:T(8,128)(2,1)}), bf16[768,6144]{1,0:T(8,128)(2,1)}) %all-gather.6.cloned.1.call-update) | async-done | bytes 9437200 | tf_op jit(solution)/shard_map/all_gather | solution.py:55
  206.5 9.6 %fusion.8 = f32[512,768]{0,1:T(8,128)S(1)} fusion(bf16[512,6144]{1,0:T(8,128)(2,1)} %param.15, bf16[768,6144]{1,0:T(8,128)(2,1)} %all-gather.6.cloned.1.call-done), kind=kOutput, calls=%fused_computation.27 | convolution fusion | flops 4831838208 | bytes 17301504 | tf_op jit(solution)/shard_map/dot_general | solution.py:57
  216.8 1.4 fusion
  220.9 10.8 %convolution_convert_fusion = bf16[512,6144]{1,0:T(8,128)(2,1)} fusion(bf16[512,768]{0,1:T(8,128)(2,1)} %bitcast.83, bf16[768,6144]{1,0:T(8,128)(2,1)} %all-gather.6.cloned.1.call-done), kind=kOutput, calls=%fused_computation.2 | convolution fusion | flops 4834983936 | bytes 16515072 | tf_op jit(solution)/shard_map/dot_general | solution.py:56
  231.7 2.0 select_convert_fusion
  233.8 1.1 fusion.9
  234.9 1.2 fusion.2
  236.2 2.3 copy.71
  238.5 3.8 fusion.10
  242.2 1.8 fusion.11
  244.0 115.4 %all-reduce.2.cloned.1.call-done = bf16[6,128,128]{1,2,0:T(8,128)(2,1)} async-done(((bf16[6,128,128]{1,2,0:T(8,128)(2,1)}), bf16[6,128,128]{1,2,0:T(8,128)(2,1)}) %all-reduce.2.cloned.1.call-update) | async-done | bytes 196624 | tf_op jit(solution)/shard_map/psum | solution.py:88
  359.4 1.8 copy.74
  361.2 91.8 %all-gather.10.cloned.1.call-done = bf16[192,128,128]{2,1,0:T(8,128)(2,1)} async-done(((bf16[6,128,128]{2,1,0:T(8,128)(2,1)}), bf16[192,128,128]{2,1,0:T(8,128)(2,1)}) %all-gather.10.cloned.1.call-update) | async-done | bytes 6291472 | tf_op jit(solution)/shard_map/all_gather | solution.py:13
  453.0 32.2 %while.23 = (s32[]{:T(128)}, f32[6,128,128]{2,1,0:T(8,128)S(1)}, s32[]{:T(128)}, bf16[32,6,128,128]{3,2,1,0:T(8,128)(2,1)}, s32[]{:T(128)}, /*index=5*/s32[]{:T(128)}, s32[]{:T(128)}, s32[]{:T(128)}) while((s32[]{:T(128)}, f32[6,128,128]{2,1,0:T(8,128)S(1)}, s32[]{:T(128)}, bf16[32,6,128,128]{3,2,1,0:T(8,128)(2,1)}, s32[]{:T(128)}, ...), condition=%wide.region_6.7_spmd, body=%wide.region_5.6_spmd.sunk | while | flops 196614 | bytes 983183 | solution.py:20
  453.1 1.0 convert_add_fusion.5
  457.2 1.0 convert_add_fusion.5
  458.2 1.0 convert_add_fusion.5
  463.4 1.0 convert_add_fusion.5
  464.4 1.1 convert_add_fusion.5
  465.5 1.0 convert_add_fusion.5
  467.6 1.0 convert_add_fusion.5
  468.6 1.0 convert_add_fusion.5
  469.7 1.0 convert_add_fusion.5
  470.7 1.0 convert_add_fusion.5
  471.7 1.0 convert_add_fusion.5
  472.8 1.0 convert_add_fusion.5
  473.8 1.0 convert_add_fusion.5
  474.9 1.0 convert_add_fusion.5
  475.9 1.0 convert_add_fusion.5
  476.9 1.0 convert_add_fusion.5
  478.0 1.0 convert_add_fusion.5
  479.0 1.0 convert_add_fusion.5
  480.1 1.0 convert_add_fusion.5
  481.1 1.0 convert_add_fusion.5
  482.1 1.0 convert_add_fusion.5
  483.2 1.0 convert_add_fusion.5
  484.2 1.0 convert_add_fusion.5
  485.3 2.9 add_convert_fusion
  488.1 2.3 copy.73
  490.8 1.2 copy.72
  491.9 6.0 %reduce-scatter.2.cloned.1.call-done = bf16[512,768]{1,0:T(8,128)(2,1)} async-done(((bf16[512,6144]{1,0:T(8,128)(2,1)}), bf16[512,768]{1,0:T(8,128)(2,1)}) %reduce-scatter.2.cloned.1.call-update) | async-done | bytes 786448 | tf_op jit(solution)/shard_map/reduce_scatter | solution.py:60
  (46 shorter events, 13.0 us)
Async XLA Ops:
  7.2 4.8 copy-start.6
  7.2 96.3 %all-gather.8.cloned.1.call-start = ((), (), s32[]{:S(2)}) async-start(), calls=%async_computation.4 | async-start | bytes 6488064 | tf_op jit(solution)/shard_map/all_gather | solution.py:13
  11.2 195.4 %all-gather.6.cloned.1.call-start = ((), (), s32[]{:S(2)}) async-start(), calls=%async_computation.1 | async-start | bytes 9732096 | tf_op jit(solution)/shard_map/all_gather | solution.py:55
  12.3 1.1 copy-start.8
  13.4 1.7 copy-start
  17.4 86.2 %copy-start.7 = (f32[6,128,128]{2,1,0:T(8,128)S(1)}, f32[6,128,128]{2,1,0:T(8,128)}, u32[]{:S(2)}) copy-start(f32[6,128,128]{2,1,0:T(8,128)} %param.13) | copy-start | bytes 1179652
  206.5 9.6 %copy-start.4 = (f32[6,512,128]{1,2,0:T(8,128)S(1)}, f32[6,512,128]{1,2,0:T(8,128)}, u32[]{:S(2)}) copy-start(f32[6,512,128]{1,2,0:T(8,128)} %fusion.7) | copy-start | bytes 4718596
  218.5 0.8 copy-start.5
  219.4 140.0 %all-reduce.2.cloned.1.call-start = ((), (), s32[]{:S(2)}) async-start(), calls=%async_computation.3 | async-start | bytes 393216 | tf_op jit(solution)/shard_map/psum | solution.py:88
  220.1 232.9 %all-gather.10.cloned.1.call-start = ((), (), s32[]{:S(2)}) async-start(), calls=%async_computation.5 | async-start | bytes 6488064 | tf_op jit(solution)/shard_map/all_gather | solution.py:13
  220.7 277.3 %reduce-scatter.2.cloned.1.call-start = ((), (), s32[]{:S(2)}) async-start(), calls=%async_computation.2 | async-start | bytes 7077888 | tf_op jit(solution)/shard_map/reduce_scatter | solution.py:60
  233.8 2.4 copy-start.1
  238.4 3.8 copy-start.2
  485.3 5.2 %copy-start.3 = (f32[6,512,128]{1,2,0:T(8,128)S(1)}, f32[6,512,128]{1,2,0:T(8,128)}, u32[]{:S(2)}) copy-start(f32[6,512,128]{1,2,0:T(8,128)} %fusion.11) | copy-start | bytes 4718596
Sparse Core Ops, SparseCore 0:
  11.3 92.1 all-gather.7
  106.1 100.4 all-gather.5
  223.6 135.7 all-reduce.1
  362.7 90.2 all-gather.9
  456.1 41.7 reduce-scatter.1
where the time goes:
time: 506 us; the launch traced here: 504 us
  waiting for transfers between devices  404 us (80%)
  matrix products  38.9 us (8%)
  other arithmetic  33 us (7%)
  between operations  14 us (3%)
  local copies, waits for them, and re-layouts  13.3 us (3%)
    all_gather x2, waiting for transfers between devices, prefix(): gathered = lax.all_gather(value.astype(jnp.bfloat16), axis)  178 us
    psum x1, waiting for transfers between devices, shards(): lax.psum(own_adjoint.astype(jnp.bfloat16), 'seq').astype(jnp.float32)  115 us
    all_gather x1, waiting for transfers between devices, shards(): weight_rows = lax.all_gather(out_weight, 'seq', axis=0, tiled=True)  103 us
    add x31, other arithmetic, add_states(): return earlier + later  31.5 us
    unnamed x25, local copies, waits for them, and re-layouts  12.4 us
    dot_general x1, matrix products, shards(): projected = jnp.dot(normed, weight_rows, preferred_element_type=jnp.float32)  10.8 us
  transfers between devices with their start and end apart: 5, of which 5 were waited for; matrix products, arithmetic and copies ran while one was open for 13% of the time, Pallas kernels for 0%

commit v1 on v0

--- a/solution.py
+++ b/solution.py
@@ -4,6 +4,11 @@
 from jax.sharding import PartitionSpec as P
 
 EPS = 1e-06
+
+
+def all_by_exchange(array, axis, dim):
+    sent = jnp.stack([array] * lax.axis_size(axis))
+    return jnp.concatenate(lax.all_to_all(sent, axis, 0, 0), axis=dim)
 
 
 def prefix(value, axis, join, neutral, backward):
@@ -52,7 +57,7 @@
         "thi,hij->thj", queries, state_half, preferred_element_type=jnp.float32
     )
     normed = normalize(attended).astype(jnp.bfloat16).reshape(tok_rows, width)
-    weight_rows = lax.all_gather(out_weight, "seq", axis=0, tiled=True)
+    weight_rows = all_by_exchange(out_weight, "seq", 0)
     projected = jnp.dot(normed, weight_rows, preferred_element_type=jnp.float32)
     grad_normed = lax.dot_general(
         out_grad, weight_rows, (((1,), (1,)), ((), ())), preferred_element_type=jnp.float32

time: 506 us -> 579 us (1.14)
  waiting for transfers between devices: 404 us -> 461 us
  starting transfers between devices: 0.34 us -> 12.6 us
    all_gather x2, waiting for transfers between devices: 178 us -> 291 us  [prefix(): gathered = lax.all_gather(value.astype(jnp.bfloat16), axis)]
    all_gather x1 -> x0, waiting for transfers between devices: 103 us -> none  [shards(): weight_rows = lax.all_gather(out_weight, 'seq', axis=0, tiled=True)]
    all_to_all x0 -> x1, waiting for transfers between devices: none -> 32.5 us  [all_by_exchange(): return jnp.concatenate(lax.all_to_all(sent, axis, 0, 0), axis=dim)]
    psum x1, waiting for transfers between devices: 115 us -> 130 us  [shards(): lax.psum(own_adjoint.astype(jnp.bfloat16), 'seq').astype(jnp.float32)]
    all_to_all x0 -> x1, starting transfers between devices: none -> 12.3 us  [all_by_exchange(): return jnp.concatenate(lax.all_to_all(sent, axis, 0, 0), axis=dim)]
    unnamed x25 -> x27, local copies, waits for them, and re-layouts: 12.4 us -> 11.3 us
  transfers between devices with their start and end apart: 5 -> 5, of which waited for: 5 -> 5; matrix products, arithmetic and copies ran while one was open for 13% -> 12% of each run, Pallas kernels for 0% -> 0%
where the time goes in v1:
time: 579 us; the launch traced here: 578 us
  waiting for transfers between devices  461 us (80%)
  matrix products  39 us (7%)
  other arithmetic  33 us (6%)
  local copies, waits for them, and re-layouts  17.9 us (3%)
  between operations  14 us (2%)
  starting transfers between devices  12.6 us (2%)
    all_gather x2, waiting for transfers between devices, prefix(): gathered = lax.all_gather(value.astype(jnp.bfloat16), axis)  291 us
    psum x1, waiting for transfers between devices, shards(): lax.psum(own_adjoint.astype(jnp.bfloat16), 'seq').astype(jnp.float32)  130 us
    all_to_all x1, waiting for transfers between devices, all_by_exchange(): return jnp.concatenate(lax.all_to_all(sent, axis, 0, 0), axis=dim)  32.5 us
    add x31, other arithmetic, add_states(): return earlier + later  31.5 us
    all_to_all x1, starting transfers between devices, all_by_exchange(): return jnp.concatenate(lax.all_to_all(sent, axis, 0, 0), axis=dim)  12.3 us
  transfers between devices with their start and end apart: 5, of which 5 were waited for; matrix products, arithmetic and copies ran while one was open for 12% of the time, Pallas kernels for 0%

profile of v1, /device:TPU:1, one launch (start us, length us, event | category | flops | bytes accessed | tf_op | source)
XLA Modules:
  0.0 578.2 jit_solution(17032272657107158921)
XLA Ops:
  7.2 5.8 %stack.2 = bf16[32,24,6144]{2,1,0:T(8,128)(2,1)} broadcast(bf16[24,6144]{1,0:T(8,128)(2,1)} %param.14), dimensions={1,2} | broadcast | bytes 9732096 | tf_op jit(solution)/shard_map/stack | solution.py:10
  13.0 12.3 %all-to-all-start = ((bf16[32,24,6144]{2,1,0:T(8,128)(2,1)}), bf16[32,24,6144]{2,1,0:T(8,128)(2,1)}, u32[]{:S(2)}, u32[]{:S(2)}) async-start(bf16[32,24,6144]{2,1,0:T(8,128)(2,1)} %stack.2), calls=%async_computation | async-start | bytes 18874368 | tf_op jit(solution)/shard_map/all_to_all | solution.py:11
  25.9 1.0 convolution_convert_fusion.2
  27.0 1.4 copy.52
  28.5 1.1 select_convert_fusion.1
  29.6 1.7 copy-done
  31.3 2.4 fusion.9
  33.7 198.7 %all-gather.5.cloned.1.call-done = bf16[192,128,128]{2,1,0:T(8,128)(2,1)} async-done(((bf16[6,128,128]{2,1,0:T(8,128)(2,1)}), bf16[192,128,128]{2,1,0:T(8,128)(2,1)}) %all-gather.5.cloned.1.call-update) | async-done | bytes 6291472 | tf_op jit(solution)/shard_map/all_gather | solution.py:18
  232.5 32.5 %all-to-all-done = bf16[32,24,6144]{2,1,0:T(8,128)(2,1)} async-done(((bf16[32,24,6144]{2,1,0:T(8,128)(2,1)}), bf16[32,24,6144]{2,1,0:T(8,128)(2,1)}, u32[]{:S(2)}, u32[]{:S(2)}) %all-to-all-start) | async-done | bytes 9437216 | tf_op jit(solution)/shard_map/all_to_all | solution.py:11
  265.0 9.6 %fusion = f32[512,6,128]{0,2,1:T(8,128)S(1)} fusion(bf16[6,128,6144]{2,1,0:T(8,128)(2,1)} %bitcast.11, bf16[512,6144]{1,0:T(8,128)(2,1)} %param.15), kind=kOutput, calls=%fused_computation.3 | convolution fusion | flops 4831838208 | bytes 17301504 | tf_op jit(solution)/shard_map/dot_general | solution.py:62
  275.3 1.4 fusion.2
  279.5 10.8 %convolution_convert_fusion = bf16[512,6144]{1,0:T(8,128)(2,1)} fusion(bf16[512,768]{0,1:T(8,128)(2,1)} %bitcast.84, bf16[768,6144]{1,0:T(8,128)(2,1)} %bitcast.9), kind=kOutput, calls=%fused_computation.2 | convolution fusion | flops 4834983936 | bytes 16515072 | tf_op jit(solution)/shard_map/dot_general | solution.py:61
  290.4 2.0 select_convert_fusion
  292.4 1.1 fusion.10
  293.6 1.2 fusion.4
  294.8 2.3 copy.68
  297.1 3.8 fusion.12
  300.9 1.7 fusion.11
  302.6 130.3 %all-reduce.2.cloned.1.call-done = bf16[6,128,128]{1,2,0:T(8,128)(2,1)} async-done(((bf16[6,128,128]{1,2,0:T(8,128)(2,1)}), bf16[6,128,128]{1,2,0:T(8,128)(2,1)}) %all-reduce.2.cloned.1.call-update) | async-done | bytes 196624 | tf_op jit(solution)/shard_map/psum | solution.py:93
  432.9 1.8 copy.71
  434.7 92.0 %all-gather.7.cloned.1.call-done = bf16[192,128,128]{2,1,0:T(8,128)(2,1)} async-done(((bf16[6,128,128]{2,1,0:T(8,128)(2,1)}), bf16[192,128,128]{2,1,0:T(8,128)(2,1)}) %all-gather.7.cloned.1.call-update) | async-done | bytes 6291472 | tf_op jit(solution)/shard_map/all_gather | solution.py:18
  526.8 32.2 %while.23 = (s32[]{:T(128)}, f32[6,128,128]{2,1,0:T(8,128)S(1)}, s32[]{:T(128)}, bf16[32,6,128,128]{3,2,1,0:T(8,128)(2,1)}, s32[]{:T(128)}, /*index=5*/s32[]{:T(128)}, s32[]{:T(128)}, s32[]{:T(128)}) while((s32[]{:T(128)}, f32[6,128,128]{2,1,0:T(8,128)S(1)}, s32[]{:T(128)}, bf16[32,6,128,128]{3,2,1,0:T(8,128)(2,1)}, s32[]{:T(128)}, ...), condition=%wide.region_6.7_spmd, body=%wide.region_5.6_spmd.sunk | while | flops 196614 | bytes 983183 | solution.py:25
  526.8 1.0 convert_add_fusion.5
  527.8 1.0 convert_add_fusion.5
  528.9 1.0 convert_add_fusion.5
  529.9 1.0 convert_add_fusion.5
  530.9 1.0 convert_add_fusion.5
  538.2 1.1 convert_add_fusion.5
  539.3 1.0 convert_add_fusion.5
  542.4 1.0 convert_add_fusion.5
  544.4 1.0 convert_add_fusion.5
  545.5 1.0 convert_add_fusion.5
  546.5 1.0 convert_add_fusion.5
  547.5 1.0 convert_add_fusion.5
  548.6 1.0 convert_add_fusion.5
  549.6 1.0 convert_add_fusion.5
  550.7 1.0 convert_add_fusion.5
  551.7 1.0 convert_add_fusion.5
  552.7 1.0 convert_add_fusion.5
  553.8 1.0 convert_add_fusion.5
  554.8 1.0 convert_add_fusion.5
  555.9 1.0 convert_add_fusion.5
  556.9 1.0 convert_add_fusion.5
  558.0 1.0 convert_add_fusion.5
  559.0 2.8 fusion.3
  561.8 2.3 copy.69
  564.5 1.2 copy.70
  565.7 6.0 %reduce-scatter.2.cloned.1.call-done = bf16[512,768]{1,0:T(8,128)(2,1)} async-done(((bf16[512,6144]{1,0:T(8,128)(2,1)}), bf16[512,768]{1,0:T(8,128)(2,1)}) %reduce-scatter.2.cloned.1.call-update) | async-done | bytes 786448 | tf_op jit(solution)/shard_map/reduce_scatter | solution.py:65
  (48 shorter events, 13.8 us)
Async XLA Ops:
  13.0 12.3 %copy-start.6 = (bf16[512,768]{1,0:T(8,128)(2,1)S(1)}, bf16[512,768]{1,0:T(8,128)(2,1)}, u32[]{:S(2)}) copy-start(bf16[512,768]{1,0:T(8,128)(2,1)} %param.11) | copy-start | bytes 2359300
  13.0 12.6 %copy-start.7 = (bf16[512,768]{1,0:T(8,128)(2,1)S(1)}, bf16[512,768]{1,0:T(8,128)(2,1)}, u32[]{:S(2)}) copy-start(bf16[512,768]{1,0:T(8,128)(2,1)} %param.12) | copy-start | bytes 2359300
  13.0 252.1 %all-to-all-start = ((bf16[32,24,6144]{2,1,0:T(8,128)(2,1)}), bf16[32,24,6144]{2,1,0:T(8,128)(2,1)}, u32[]{:S(2)}, u32[]{:S(2)}) async-start(bf16[32,24,6144]{2,1,0:T(8,128)(2,1)} %stack.2), calls=%async_computation | async-start | bytes 18874368 | tf_op jit(solution)/shard_map/all_to_all | solution.py:11
  25.2 207.1 %all-gather.5.cloned.1.call-start = ((), (), s32[]{:S(2)}) async-start(), calls=%async_computation.4 | async-start | bytes 6488064 | tf_op jit(solution)/shard_map/all_gather | solution.py:18
  28.5 1.1 copy-start.9
  29.6 1.7 copy-start
  33.7 198.7 %copy-start.8 = (f32[6,128,128]{2,1,0:T(8,128)S(1)}, f32[6,128,128]{2,1,0:T(8,128)}, u32[]{:S(2)}) copy-start(f32[6,128,128]{2,1,0:T(8,128)} %param.13) | copy-start | bytes 1179652
  265.0 9.6 %copy-start.4 = (f32[6,512,128]{1,2,0:T(8,128)S(1)}, f32[6,512,128]{1,2,0:T(8,128)}, u32[]{:S(2)}) copy-start(f32[6,512,128]{1,2,0:T(8,128)} %fusion.9) | copy-start | bytes 4718596
  277.0 0.8 copy-start.5
  277.8 155.1 %all-reduce.2.cloned.1.call-start = ((), (), s32[]{:S(2)}) async-start(), calls=%async_computation.3 | async-start | bytes 393216 | tf_op jit(solution)/shard_map/psum | solution.py:93
  278.6 248.2 %all-gather.7.cloned.1.call-start = ((), (), s32[]{:S(2)}) async-start(), calls=%async_computation.5 | async-start | bytes 6488064 | tf_op jit(solution)/shard_map/all_gather | solution.py:18
  279.3 292.4 %reduce-scatter.2.cloned.1.call-start = ((), (), s32[]{:S(2)}) async-start(), calls=%async_computation.2 | async-start | bytes 7077888 | tf_op jit(solution)/shard_map/reduce_scatter | solution.py:65
  292.4 2.4 copy-start.2
  297.1 3.8 copy-start.1
  559.0 5.1 copy-start.3
Sparse Core Ops, SparseCore 0:
  29.2 203.0 all-gather.4
  282.1 150.8 all-reduce.1
  436.4 90.2 all-gather.6
  529.9 41.7 reduce-scatter.1
